TPU v7x, 32 devices: a whole 2x2x4 slice. The times are simulated.
32 devices in a mesh: dp: 8 (over z, x), seq: 4 (over y, core).
Axes of the slice: x: 2, y: 2, z: 4, core: 2. Of those that a mesh axis runs over, the one named last changes fastest.
Arguments:
- inputs: bfloat16 [32, 1024, 1024], P('dp', 'seq'), may hold values from -6 to 6
- norm_gain: float32 [1024], replicated, may hold values from 0.1 to 1.9
- norm_shift: float32 [1024], replicated, may hold values from -3 to 3
- qkv_weight: bfloat16 [1024, 3072], replicated, may hold values from -0.1875 to 0.1875
- out_weight: bfloat16 [1024, 1024], replicated, may hold values from -0.75 to 0.75
- up_weight: bfloat16 [1024, 4096], replicated, may hold values from -0.1875 to 0.1875
- up_bias: float32 [4096], replicated, may hold values from -3 to 3
- down_weight: bfloat16 [4096, 1024], replicated, may hold values from -0.09375 to 0.09375
- down_bias: float32 [1024], replicated, may hold values from -3 to 3
- partners: int32 [32], P('dp'), may hold values from 0 to 31, as said below
- families: int32 [32, 1024], P('dp'), may hold values from 0 to 1023, as said below
- cotangent: bfloat16 [32, 1024, 1024], P('dp', 'seq'), may hold values from -6 to 6
Outputs:
- layer_out: bfloat16 [32, 1024, 1024], P('dp', 'seq')
- input_grad: float32 [32, 1024, 1024], P('dp', 'seq')
- gain_grad: float32 [1024], replicated
- shift_grad: float32 [1024], replicated
- qkv_grad: float32 [1024, 3072], P('dp', 'seq')
- out_grad: float32 [1024, 1024], P('dp', 'seq')
- up_grad: float32 [1024, 4096], P('dp', 'seq')
- up_bias_grad: float32 [4096], replicated
- down_grad: float32 [4096, 1024], P('dp', 'seq')
- down_bias_grad: float32 [1024], replicated
Inputs may be any that keep to these rules, and one draw needn't show every extreme that they name: partners pairs the rows of each aligned block of 4 rows two by two: partners[partners[r]] = r, partners[r] != r, and partners[r] lies in the block of r. `families`: family ids never fall along a row and the last position of every row has id 1024 - 1; in each aligned block of 4 rows at least one row is a single group over all 1024 positions.
All inputs are finite; a program needn't handle non-finite values.
Results may differ from a plain program's by a relative error of at most 0.0099.
Values may be sent and summed in bfloat16 or wider, within the bound.
A program may use at most 256 MiB of HBM per device.

v0:
```python
import jax
import jax.numpy as jnp
from jax import lax
from jax.sharding import PartitionSpec as P

HEADS = 16
HEAD_DIM = 64
ROT = 32
EPS = 1e-05


def norm_piece(values, norm_gain, norm_shift):
    row_mean = jnp.mean(values, -1, keepdims=True)
    centered = values - row_mean
    variance = jnp.mean(centered * centered, -1, keepdims=True)
    return centered * lax.rsqrt(variance + EPS) * norm_gain + norm_shift


def rotate(values, places):
    half_rot = ROT // 2
    inverse_freq = 10000.0 ** (-2.0 * jnp.arange(half_rot).astype(jnp.float32) / ROT)
    angles = places.astype(jnp.float32)[:, None] * inverse_freq[None, :]
    cosine_table = jnp.cos(angles)[:, None, :]
    sine_table = jnp.sin(angles)[:, None, :]
    first_half = values[..., :half_rot]
    second_half = values[..., half_rot:ROT]
    return jnp.concatenate(
        [
            first_half * cosine_table - second_half * sine_table,
            second_half * cosine_table + first_half * sine_table,
            values[..., ROT:],
        ],
        -1,
    )


def gelu_piece(values):
    return jax.nn.gelu(values, approximate=True)


def masked_scores(queries, key_rows, family):
    scaling = HEAD_DIM ** (-0.5)
    scores = (
        jnp.einsum("qhd,khd->hqk", queries, key_rows, preferred_element_type=jnp.float32) * scaling
    )
    places = jnp.arange(queries.shape[0])
    allowed = (places[None, :] <= places[:, None]) & (family[:, None] == family[None, :])
    return jnp.where(allowed[None], scores, -1000000000.0)


def forward_row(pieces):
    qkv_rows, family = pieces
    scores = masked_scores(qkv_rows[:, 0], qkv_rows[:, 1], family)
    row_max = jnp.max(scores, -1, keepdims=True)
    weights = jnp.exp(scores - row_max)
    row_total = jnp.sum(weights, -1, keepdims=True)
    prob_low = (weights / row_total).astype(jnp.bfloat16)
    mixed_heads = jnp.einsum(
        "hqk,khd->qhd", prob_low, qkv_rows[:, 2], preferred_element_type=jnp.float32
    )
    return (mixed_heads.astype(jnp.bfloat16), (row_max + jnp.log(row_total))[..., 0])


def backward_row(pieces):
    qkv_rows, family, log_total, d_mixed = pieces
    scaling = HEAD_DIM ** (-0.5)
    queries = qkv_rows[:, 0]
    key_rows = qkv_rows[:, 1]
    value_rows = qkv_rows[:, 2]
    scores = masked_scores(queries, key_rows, family)
    chances = jnp.exp(scores - log_total[..., None])
    d_chances = jnp.einsum("qhd,khd->hqk", d_mixed, value_rows, preferred_element_type=jnp.float32)
    d_scores = (chances * (d_chances - jnp.sum(chances * d_chances, -1, keepdims=True))).astype(
        jnp.bfloat16
    )
    d_value = jnp.einsum(
        "hqk,qhd->khd", chances.astype(jnp.bfloat16), d_mixed, preferred_element_type=jnp.float32
    )
    d_query = (
        jnp.einsum("hqk,khd->qhd", d_scores, key_rows, preferred_element_type=jnp.float32) * scaling
    )
    d_key = (
        jnp.einsum("hqk,qhd->khd", d_scores, queries, preferred_element_type=jnp.float32) * scaling
    )
    return jnp.stack([d_query, d_key, d_value], 1).astype(jnp.bfloat16)


def on_device(
    inputs,
    norm_gain,
    norm_shift,
    qkv_weight,
    out_weight,
    up_weight,
    up_bias,
    down_weight,
    down_bias,
    partners,
    families,
    cotangent,
):
    row_count, place_count, model_width = inputs.shape
    seq_size = lax.axis_size("seq")
    token_count = row_count * place_count
    values = inputs.astype(jnp.float32)
    normed, norm_pull = jax.vjp(norm_piece, values, norm_gain, norm_shift)
    normed_low = normed.astype(jnp.bfloat16).reshape(token_count, model_width)
    raw_qkv = jnp.dot(normed_low, qkv_weight, preferred_element_type=jnp.float32)
    raw_qkv = raw_qkv.reshape(row_count, place_count, 3, HEADS, HEAD_DIM)
    places = lax.axis_index("seq") * place_count + jnp.arange(place_count)

    def rope_piece(raw_values):
        return jnp.stack(
            [
                rotate(raw_values[:, :, 0], places),
                rotate(raw_values[:, :, 1], places),
                raw_values[:, :, 2],
            ],
            2,
        )

    rotated, rope_pull = jax.vjp(rope_piece, raw_qkv)
    outgoing = rotated.astype(jnp.bfloat16).reshape(row_count, place_count, 3, seq_size, -1)
    received = lax.all_to_all(outgoing, "seq", split_axis=3, concat_axis=1, tiled=True)
    full_length = received.shape[1]
    received = received.reshape(row_count, full_length, 3, -1, HEAD_DIM)
    mixed_heads, log_totals = lax.map(forward_row, (received, families))
    group_width = mixed_heads.shape[2] * HEAD_DIM
    returned = lax.all_to_all(
        mixed_heads.reshape(row_count, full_length, 1, group_width),
        "seq",
        split_axis=1,
        concat_axis=2,
        tiled=True,
    )
    heads_low = returned.reshape(token_count, model_width)
    attn_out = jnp.dot(heads_low, out_weight, preferred_element_type=jnp.float32)
    hidden = jnp.dot(normed_low, up_weight, preferred_element_type=jnp.float32) + up_bias
    active, gelu_pull = jax.vjp(gelu_piece, hidden)
    active_low = active.astype(jnp.bfloat16)
    mlp_out = jnp.dot(active_low, down_weight, preferred_element_type=jnp.float32) + down_bias
    layer_out = (
        (values.reshape(token_count, model_width) + attn_out + mlp_out)
        .astype(jnp.bfloat16)
        .reshape(inputs.shape)
    )
    local_rows = partners - lax.axis_index("dp") * row_count
    grad_low = jnp.take(cotangent, local_rows, axis=0).reshape(token_count, model_width)
    down_grad = jnp.einsum("tf,td->fd", active_low, grad_low, preferred_element_type=jnp.float32)
    down_bias_grad = jnp.sum(grad_low.astype(jnp.float32), 0)
    out_grad = jnp.einsum("te,td->ed", heads_low, grad_low, preferred_element_type=jnp.float32)
    d_active = jnp.einsum("td,fd->tf", grad_low, down_weight, preferred_element_type=jnp.float32)
    d_hidden_low = gelu_pull(d_active)[0].astype(jnp.bfloat16)
    up_bias_grad = jnp.sum(d_hidden_low.astype(jnp.float32), 0)
    up_grad = jnp.einsum("td,tf->df", normed_low, d_hidden_low, preferred_element_type=jnp.float32)
    d_heads = jnp.einsum(
        "td,ed->te", grad_low, out_weight, preferred_element_type=jnp.float32
    ).astype(jnp.bfloat16)
    d_heads = d_heads.reshape(row_count, place_count, seq_size, group_width)
    d_heads_split = lax.all_to_all(d_heads, "seq", split_axis=2, concat_axis=1, tiled=True)
    d_heads_split = d_heads_split.reshape(row_count, full_length, -1, HEAD_DIM)
    d_blocks = lax.map(backward_row, (received, families, log_totals, d_heads_split))
    d_blocks = d_blocks.reshape(row_count, full_length, 3, 1, group_width)
    d_rotated = lax.all_to_all(d_blocks, "seq", split_axis=1, concat_axis=3, tiled=True)
    d_rotated = d_rotated.reshape(row_count, place_count, 3, HEADS, HEAD_DIM).astype(jnp.float32)
    d_raw_low = rope_pull(d_rotated)[0].astype(jnp.bfloat16).reshape(token_count, 3 * model_width)
    qkv_grad = jnp.einsum("td,te->de", normed_low, d_raw_low, preferred_element_type=jnp.float32)
    d_normed = jnp.einsum("te,de->td", d_raw_low, qkv_weight, preferred_element_type=jnp.float32)
    d_normed = d_normed + jnp.einsum(
        "tf,df->td", d_hidden_low, up_weight, preferred_element_type=jnp.float32
    )
    d_values, gain_grad, shift_grad = norm_pull(d_normed.reshape(inputs.shape))
    input_grad = grad_low.astype(jnp.float32).reshape(inputs.shape) + d_values
    gain_sum, shift_sum, up_bias_sum, down_bias_sum = lax.psum(
        (gain_grad, shift_grad, up_bias_grad, down_bias_grad), ("dp", "seq")
    )
    partial_sums = (
        lax.psum_scatter(qkv_grad, "seq", scatter_dimension=1, tiled=True),
        lax.psum_scatter(out_grad, "seq", scatter_dimension=1, tiled=True),
        lax.psum_scatter(up_grad, "seq", scatter_dimension=1, tiled=True),
        lax.psum_scatter(down_grad, "seq", scatter_dimension=1, tiled=True),
    )
    qkv_sum, out_sum, up_sum, down_sum = (
        lax.psum_scatter(partial_sums[0], "dp", scatter_dimension=0, tiled=True),
        lax.psum_scatter(partial_sums[1], "dp", scatter_dimension=0, tiled=True),
        lax.psum_scatter(partial_sums[2], "dp", scatter_dimension=0, tiled=True),
        lax.psum_scatter(partial_sums[3], "dp", scatter_dimension=0, tiled=True),
    )
    return (
        layer_out,
        input_grad,
        gain_sum,
        shift_sum,
        qkv_sum,
        out_sum,
        up_sum,
        up_bias_sum,
        down_sum,
        down_bias_sum,
    )


def solution(mesh):
    placed = (
        P("dp", "seq", None),
        P(),
        P(),
        P(),
        P(),
        P(),
        P(),
        P(),
        P(),
        P("dp"),
        P("dp", None),
        P("dp", "seq", None),
    )
    return jax.shard_map(
        on_device,
        mesh=mesh,
        in_specs=placed,
        out_specs=(
            P("dp", "seq", None),
            P("dp", "seq", None),
            P(),
            P(),
            P("dp", "seq"),
            P("dp", "seq"),
            P("dp", "seq"),
            P(),
            P("dp", "seq"),
            P(),
        ),
        check_vma=False,
    )
```

profile of v0, /device:TPU:0, one launch (start us, length us, event | category | flops | bytes accessed | tf_op | source)
XLA Modules:
  0.0 1331.5 jit_solution(15439892296866444212)
XLA Ops:
  36.0 8.7 copy.107
  48.4 10.8 fusion.39
  78.0 5.8 all-to-all-start
  96.9 58.3 %all-to-all-done = bf16[4,256,3,4,256]{1,4,0,2,3:T(8,128)(2,1)} async-done(((bf16[4,256,3,4,256]{1,4,0,2,3:T(8,128)(2,1)}), bf16[4,256,3,4,256]{1,4,0,2,3:T(8,128)(2,1)}, u32[]{:S(2)}, u32[]{:S(2)}) %all-to-all-start) | async-done | bytes 6291488 | tf_op jit(solution)/shard_map/all_to_all | solution.py:124
  155.2 10.3 copy.112
  165.4 11.0 reshape.385
  176.4 60.7 %while.22 = (s32[]{:T(128)}, bf16[4,1024,4,64]{1,3,2,0:T(8,128)(2,1)}, f32[4,4,1024]{2,1,0:T(4,128)}, bf16[4,1024,3,4,64]{1,4,3,2,0:T(8,128)(2,1)}, s32[4,1024]{1,0:T(4,128)S(1)}, /*index=5*/s32[]{:T(128)}) while((s32[]{:T(128)}, bf16[4,1024,4,64]{1,3,2,0:T(8,128)(2,1)}, f32[4,4,1024]{2,1,0:T(4,128)}, bf16[4,1024,3,4,64]{1,4,3,2,0:T(8,128)(2,1)}, ...), condition=%wide.region_5.6_spmd, body=%wide.region_2.5_spmd.sunk | while | flops 1127477248 | bytes 59913292 | solution.py:127
  186.0 5.6 fusion.93
  201.2 5.6 fusion.93
  216.3 5.6 fusion.93
  231.5 5.6 fusion.93
  246.0 208.5 %while.23 = (s32[]{:T(128)}, bf16[4,1024,3,4,64]{1,4,3,2,0:T(8,128)(2,1)}, bf16[4,1024,3,4,64]{1,4,3,2,0:T(8,128)(2,1)}, s32[4,1024]{1,0:T(4,128)S(1)}, f32[4,4,...) while((s32[]{:T(128)}, bf16[4,1024,3,4,64]{1,4,3,2,0:T(8,128)(2,1)}, ...), condition=%wide.region_8.9_spmd, body=%wide.region_6.8_spmd.sunk | while | flops 2731274240 | bytes 196179696 | solution.py:162
  247.6 9.6 fusion.99
  258.5 12.7 multiply_reduce_fusion.5
  271.2 11.9 multiply_convert_fusion.5
  299.7 9.6 fusion.99
  310.6 12.7 multiply_reduce_fusion.5
  323.3 11.9 multiply_convert_fusion.5
  351.8 9.6 fusion.99
  362.7 12.7 multiply_reduce_fusion.5
  375.4 11.9 multiply_convert_fusion.5
  403.9 9.6 fusion.99
  414.8 12.7 multiply_reduce_fusion.5
  427.5 11.9 multiply_convert_fusion.5
  454.5 10.8 copy.118
  480.8 82.8 %all-to-all-done.3 = bf16[4,1024,3,1,256]{4,0,3,2,1:T(4,128)(2,1)} async-done(((bf16[4,1024,3,1,256]{4,0,3,2,1:T(4,128)(2,1)}), bf16[4,1024,3,1,256]{4,0,3,2,1:T(4,128)(2,1)}, u32[]{:S(2)}, u32[]{:S(2)}) %all-to-all-start.3) | async-done | bytes 6291488 | tf_op jit(solution)/shard_map/all_to_all | solution.py:164
  567.4 6.2 convert_bitcast_fusion
  573.6 12.6 copy.120
  586.2 9.9 fusion.45
  602.5 7.1 add_convert_fusion
  609.6 11.5 copy.121
  628.8 9.3 fusion.50
  638.2 18.6 %fusion.48 = f32[1024,4096]{1,0:T(8,128)} fusion(bf16[1024,1024]{1,0:T(8,128)(2,1)} %bitcast.215, bf16[1024,4096]{1,0:T(8,128)(2,1)} %param.21), kind=kOutput, calls=%fused_computation.117 | convolution fusion | flops 8589934592 | bytes 27262976 | tf_op jit(solution)/shard_map/dot_general | solution.py:138
  656.8 26.5 %convert_reduce_fusion = (f32[4096]{0:T(1024)S(1)}, bf16[1024,4096]{1,0:T(8,128)(2,1)}) fusion(f32[1024,4096]{1,0:T(8,128)} %fusion.48, f32[4096]{0:T(1024)S(1)} %copy-done.28, bf16[1024,1024]{1,0:T(8,128)(2,1)} %copy-done.9, bf16[4096,1024]{1,0:T(8,128)(2,1)} %param.23), kind=kOutput, calls=%fused_computation.59 | convolution fusion | flops 8686399488 | bytes 35684352 | tf_op jit(solution)/shard_map/td,fd->tf/dot_general | solution.py:152
  683.3 16.3 %fusion.52 = f32[1024,4096]{1,0:T(8,128)} fusion(bf16[1024,1024]{1,0:T(8,128)(2,1)} %bitcast.216, bf16[1024,4096]{1,0:T(8,128)(2,1)} %get-tuple-element.104), kind=kOutput, calls=%fused_computation.121 | convolution fusion | flops 8589934592 | bytes 27262976 | tf_op jit(solution)/shard_map/td,tf->df/dot_general | solution.py:155
  699.7 20.1 %fusion.43 = f32[4096,1024]{1,0:T(8,128)} fusion(bf16[1024,1024]{1,0:T(8,128)(2,1)} %copy-done.9, f32[1024,4096]{1,0:T(8,128)} %fusion.48, f32[4096]{0:T(1024)S(1)} %copy-done.28), kind=kOutput, calls=%fused_computation.113 | convolution fusion | flops 8631877632 | bytes 35667968 | tf_op jit(solution)/shard_map/tf,td->fd/dot_general | solution.py:149
  720.5 17.9 %reduce-scatter.9.cloned.1.call-done = f32[1024,768]{1,0:T(8,128)} async-done(((f32[1024,3072]{1,0:T(8,128)}), f32[1024,768]{1,0:T(8,128)}) %reduce-scatter.9.cloned.1.call-update) | async-done | bytes 3145744 | tf_op jit(solution)/shard_map/reduce_scatter | solution.py:178
  738.5 128.8 %reduce-scatter.17.cloned.1.call-done = f32[1024,1024]{1,0:T(8,128)} async-done(((f32[1024,4096]{1,0:T(8,128)}), f32[1024,1024]{1,0:T(8,128)}) %reduce-scatter.17.cloned.1.call-update) | async-done | bytes 4194320 | tf_op jit(solution)/shard_map/reduce_scatter | solution.py:180
  867.4 5.9 fusion.47
  873.3 122.5 %reduce-scatter.21.cloned.1.call-done = f32[4096,256]{1,0:T(8,128)} async-done(((f32[4096,1024]{1,0:T(8,128)}), f32[4096,256]{1,0:T(8,128)}) %reduce-scatter.21.cloned.1.call-update) | async-done | bytes 4194320 | tf_op jit(solution)/shard_map/reduce_scatter | solution.py:181
  995.9 19.7 %fusion.38 = bf16[1024,1024]{1,0:T(8,128)(2,1)} fusion(f32[1024,1024]{1,0:T(8,128)} %fusion.47, bf16[4,256,1024]{2,1,0:T(8,128)(2,1)} %param.16, f32[1024]{0:T(1024)S(1)} %copy-done.29, bf16[4096,1024]{1,0:T(8,128)(2,1)} %param.23, f32[1024,4096]{1,0:T(8,128)} %fusion.48, f32[4096]{0:T(1024)S(1)} %copy-done.28), kind=kOutput, calls=%fused_computation.74 | convolution fusion | flops 8637120512 | bytes 33574912 | tf_op jit(solution)/shard_map/dot_general | solution.py:141
  1015.5 10.7 fusion.49
  1026.3 14.2 %fusion.46 = (f32[1024]{0:T(1024)S(1)}, f32[1024,1024]{1,0:T(8,128)S(1)}) fusion(f32[1024,1024]{1,0:T(8,128)S(1)} %fusion.49, bf16[1024,4096]{1,0:T(8,128)(2,1)} %get-tuple-element.104, bf16[1024,4096]{1,0:T(8,128)(2,1)} %param.21), kind=kOutput, calls=%fused_computation.115 | convolution fusion | flops 8592030720 | bytes 25169920 | tf_op jit(solution)/shard_map/tf,df->td/dot_general | solution.py:169
  1043.5 40.4 %all-reduce.9 = (f32[1024]{0:T(1024)}, f32[1024]{0:T(1024)}, f32[4096]{0:T(1024)}, f32[1024]{0:T(1024)}) all-reduce(f32[1024]{0:T(1024)S(1)} %get-tuple-element.73, f32[1024]{0:T(1024)S(1)} %get-tuple-element.130, f32[4096]{0:T(1024)S(1)} %get-tuple-element.103, f32[1024]{0:T(1024)S(1)} %copy-done.26), channel_id=1, replica_groups=mesh['dp'=8,'seq'=4] {'dp','seq'}, use_global_device_ids=true, to_apply=%region_12.13 | all-reduce | flops 7168 | bytes 57344 | tf_op jit(solution)/shard_map/psum | solution.py:174
  1083.9 5.7 convert_add_fusion
  1089.6 51.3 %reduce-scatter.11.cloned.1.call-done = f32[128,768]{1,0:T(8,128)} async-done(((f32[1024,768]{1,0:T(8,128)}), f32[128,768]{1,0:T(8,128)}) %reduce-scatter.11.cloned.1.call-update) | async-done | bytes 393232 | tf_op jit(solution)/shard_map/reduce_scatter | solution.py:184
  1140.9 91.2 %reduce-scatter.19.cloned.1.call-done = f32[128,1024]{1,0:T(8,128)} async-done(((f32[1024,1024]{1,0:T(8,128)}), f32[128,1024]{1,0:T(8,128)}) %reduce-scatter.19.cloned.1.call-update) | async-done | bytes 524304 | tf_op jit(solution)/shard_map/reduce_scatter | solution.py:186
  1232.1 92.3 %reduce-scatter.23.cloned.1.call-done = f32[512,256]{1,0:T(8,128)} async-done(((f32[4096,256]{1,0:T(8,128)}), f32[512,256]{1,0:T(8,128)}) %reduce-scatter.23.cloned.1.call-update) | async-done | bytes 524304 | tf_op jit(solution)/shard_map/reduce_scatter | solution.py:187
  (228 shorter events, 219.8 us)
Async XLA Ops:
  7.2 7.7 copy-start
  26.4 51.6 %all-to-all-start.2 = ((bf16[4,256,4,256]{3,1,0,2:T(8,128)(2,1)}), bf16[4,256,4,256]{3,1,0,2:T(8,128)(2,1)}, u32[]{:S(2)}, u32[]{:S(2)}) async-start(bf16[4,256,4,256]{3,1,0,2:T(8,128)(2,1)} %copy.116), calls=%async_computation.2 | async-start | bytes 4194304 | tf_op jit(solution)/shard_map/all_to_all | solution.py:160
  33.1 11.6 copy-start.17
  36.0 8.7 copy-start.20
  36.0 8.7 copy-start.22
  36.0 8.7 copy-start.27
  69.3 3.2 copy-start.8
  69.5 3.0 copy-start.13
  69.5 3.0 copy-start.15
  78.0 77.2 %all-to-all-start = ((bf16[4,256,3,4,256]{1,4,0,2,3:T(8,128)(2,1)}), bf16[4,256,3,4,256]{1,4,0,2,3:T(8,128)(2,1)}, u32[]{:S(2)}, u32[]{:S(2)}) async-start(bf16[4,256,3,4,256]{1,4,0,2,3:T(8,128)(2,1)} %copy.127), calls=%async_computation | async-start | bytes 12582912 | tf_op jit(solution)/shard_map/all_to_all | solution.py:124
  165.4 11.0 copy-start.19
  241.4 223.9 %all-to-all-start.1 = ((bf16[4,1024,1,256]{3,0,2,1:T(4,128)(2,1)}), bf16[4,1024,1,256]{3,0,2,1:T(4,128)(2,1)}, u32[]{:S(2)}, u32[]{:S(2)}) async-start(bf16[4,1024,1,256]{3,0,2,1:T(4,128)(2,1)} %copy.113), calls=%async_computation.1 | async-start | bytes 4194304 | tf_op jit(solution)/shard_map/all_to_all | solution.py:129
  247.6 10.9 copy-start.1
  271.2 20.0 %slice-start = ((s8[16777216]{0:T(1024)(128)(4,1)}), s8[4194304]{0:T(1024)(128)(4,1)S(1)}, s32[]{:S(2)}) async-start(s8[16777216]{0:T(1024)(128)(4,1)} %bitcast.198), calls=%async_computation.20 | async-start | bytes 8388608 | tf_op jit(solution)/shard_map/while
  271.2 20.0 %slice-start.1 = ((s8[16777216]{0:T(1024)(128)(4,1)}), s8[4194304]{0:T(1024)(128)(4,1)S(1)}, s32[]{:S(2)}) async-start(s8[16777216]{0:T(1024)(128)(4,1)} %bitcast.198), calls=%async_computation.21 | async-start | bytes 8388608 | tf_op jit(solution)/shard_map/while
  271.2 20.0 %slice-start.2 = ((s8[16777216]{0:T(1024)(128)(4,1)}), s8[4194304]{0:T(1024)(128)(4,1)S(1)}, s32[]{:S(2)}) async-start(s8[16777216]{0:T(1024)(128)(4,1)} %bitcast.198), calls=%async_computation.22 | async-start | bytes 8388608 | tf_op jit(solution)/shard_map/while
  283.1 8.1 slice-start.3
  299.7 10.9 copy-start.1
  323.2 20.0 %slice-start = ((s8[16777216]{0:T(1024)(128)(4,1)}), s8[4194304]{0:T(1024)(128)(4,1)S(1)}, s32[]{:S(2)}) async-start(s8[16777216]{0:T(1024)(128)(4,1)} %bitcast.198), calls=%async_computation.20 | async-start | bytes 8388608 | tf_op jit(solution)/shard_map/while
  323.3 20.0 %slice-start.1 = ((s8[16777216]{0:T(1024)(128)(4,1)}), s8[4194304]{0:T(1024)(128)(4,1)S(1)}, s32[]{:S(2)}) async-start(s8[16777216]{0:T(1024)(128)(4,1)} %bitcast.198), calls=%async_computation.21 | async-start | bytes 8388608 | tf_op jit(solution)/shard_map/while
  323.3 20.0 %slice-start.2 = ((s8[16777216]{0:T(1024)(128)(4,1)}), s8[4194304]{0:T(1024)(128)(4,1)S(1)}, s32[]{:S(2)}) async-start(s8[16777216]{0:T(1024)(128)(4,1)} %bitcast.198), calls=%async_computation.22 | async-start | bytes 8388608 | tf_op jit(solution)/shard_map/while
  335.2 8.1 slice-start.3
  351.8 10.9 copy-start.1
  375.4 20.0 %slice-start = ((s8[16777216]{0:T(1024)(128)(4,1)}), s8[4194304]{0:T(1024)(128)(4,1)S(1)}, s32[]{:S(2)}) async-start(s8[16777216]{0:T(1024)(128)(4,1)} %bitcast.198), calls=%async_computation.20 | async-start | bytes 8388608 | tf_op jit(solution)/shard_map/while
  375.4 20.0 %slice-start.1 = ((s8[16777216]{0:T(1024)(128)(4,1)}), s8[4194304]{0:T(1024)(128)(4,1)S(1)}, s32[]{:S(2)}) async-start(s8[16777216]{0:T(1024)(128)(4,1)} %bitcast.198), calls=%async_computation.21 | async-start | bytes 8388608 | tf_op jit(solution)/shard_map/while
  375.4 20.0 %slice-start.2 = ((s8[16777216]{0:T(1024)(128)(4,1)}), s8[4194304]{0:T(1024)(128)(4,1)S(1)}, s32[]{:S(2)}) async-start(s8[16777216]{0:T(1024)(128)(4,1)} %bitcast.198), calls=%async_computation.22 | async-start | bytes 8388608 | tf_op jit(solution)/shard_map/while
  387.3 8.1 slice-start.3
  403.9 10.9 copy-start.1
  427.5 20.0 %slice-start = ((s8[16777216]{0:T(1024)(128)(4,1)}), s8[4194304]{0:T(1024)(128)(4,1)S(1)}, s32[]{:S(2)}) async-start(s8[16777216]{0:T(1024)(128)(4,1)} %bitcast.198), calls=%async_computation.20 | async-start | bytes 8388608 | tf_op jit(solution)/shard_map/while
  427.5 20.0 %slice-start.1 = ((s8[16777216]{0:T(1024)(128)(4,1)}), s8[4194304]{0:T(1024)(128)(4,1)S(1)}, s32[]{:S(2)}) async-start(s8[16777216]{0:T(1024)(128)(4,1)} %bitcast.198), calls=%async_computation.21 | async-start | bytes 8388608 | tf_op jit(solution)/shard_map/while
  427.5 20.0 %slice-start.2 = ((s8[16777216]{0:T(1024)(128)(4,1)}), s8[4194304]{0:T(1024)(128)(4,1)S(1)}, s32[]{:S(2)}) async-start(s8[16777216]{0:T(1024)(128)(4,1)} %bitcast.198), calls=%async_computation.22 | async-start | bytes 8388608 | tf_op jit(solution)/shard_map/while
  439.4 8.1 slice-start.3
  465.2 98.4 %all-to-all-start.3 = ((bf16[4,1024,3,1,256]{4,0,3,2,1:T(4,128)(2,1)}), bf16[4,1024,3,1,256]{4,0,3,2,1:T(4,128)(2,1)}, u32[]{:S(2)}, u32[]{:S(2)}) async-start(bf16[4,1024,3,1,256]{4,0,3,2,1:T(4,128)(2,1)} %copy.118), calls=%async_computation.3 | async-start | bytes 12582912 | tf_op jit(solution)/shard_map/all_to_all | solution.py:164
  470.5 249.4 %reduce-scatter.13.cloned.1.call-start = ((), (), s32[]{:S(2)}) async-start(), calls=%async_computation.14 | async-start | bytes 5242880 | tf_op jit(solution)/shard_map/reduce_scatter | solution.py:179
  472.8 3.5 copy-start.5
  480.8 257.6 %reduce-scatter.9.cloned.1.call-start = ((), (), s32[]{:S(2)}) async-start(), calls=%async_computation.12 | async-start | bytes 15728640 | tf_op jit(solution)/shard_map/reduce_scatter | solution.py:178
  621.2 7.6 copy-start.11
  638.1 18.7 %copy-start.28 = (f32[4096]{0:T(1024)S(1)}, f32[4096]{0:T(1024)}, u32[]{:S(2)}) copy-start(f32[4096]{0:T(1024)} %param.22) | copy-start | bytes 49156
  638.1 229.2 %reduce-scatter.17.cloned.1.call-start = ((), (), s32[]{:S(2)}) async-start(), calls=%async_computation.16 | async-start | bytes 20971520 | tf_op jit(solution)/shard_map/reduce_scatter | solution.py:180
  699.7 296.2 %reduce-scatter.21.cloned.1.call-start = ((), (), s32[]{:S(2)}) async-start(), calls=%async_computation.18 | async-start | bytes 20971520 | tf_op jit(solution)/shard_map/reduce_scatter | solution.py:181
  719.8 369.7 %reduce-scatter.15.cloned.1.call-start = ((), (), s32[]{:S(2)}) async-start(), calls=%async_computation.15 | async-start | bytes 1179648 | tf_op jit(solution)/shard_map/reduce_scatter | solution.py:185
  720.4 420.5 %reduce-scatter.11.cloned.1.call-start = ((), (), s32[]{:S(2)}) async-start(), calls=%async_computation.13 | async-start | bytes 3538944 | tf_op jit(solution)/shard_map/reduce_scatter | solution.py:184
  738.4 493.7 %reduce-scatter.19.cloned.1.call-start = ((), (), s32[]{:S(2)}) async-start(), calls=%async_computation.17 | async-start | bytes 4718592 | tf_op jit(solution)/shard_map/reduce_scatter | solution.py:186
  867.3 457.1 %reduce-scatter.23.cloned.1.call-start = ((), (), s32[]{:S(2)}) async-start(), calls=%async_computation.19 | async-start | bytes 4718592 | tf_op jit(solution)/shard_map/reduce_scatter | solution.py:187
  873.3 122.6 %copy-start.29 = (f32[1024]{0:T(1024)S(1)}, f32[1024]{0:T(1024)}, u32[]{:S(2)}) copy-start(f32[1024]{0:T(1024)} %param.24) | copy-start | bytes 12292
  1026.3 14.2 %copy-start.2 = (bf16[4,256,1024]{2,1,0:T(8,128)(2,1)S(1)}, bf16[4,256,1024]{2,1,0:T(8,128)(2,1)}, u32[]{:S(2)}) copy-start(bf16[4,256,1024]{2,1,0:T(8,128)(2,1)} %param.16) | copy-start | bytes 6291460
  1026.3 14.2 %copy-start.18 = (f32[4,256]{1,0:T(4,128)S(1)}, f32[4,256]{1,0:T(4,128)}, u32[]{:S(2)}) copy-start(f32[4,256]{1,0:T(4,128)} %copy-done.17) | copy-start | bytes 12292
  1026.3 14.2 %copy-start.23 = (f32[1024]{0:T(1024)S(1)}, f32[1024]{0:T(1024)}, u32[]{:S(2)}) copy-start(f32[1024]{0:T(1024)} %param.17) | copy-start | bytes 12292
  (13 other events, 24.2 us)
Sparse Core Ops, SparseCore 0:
  480.9 69.5 reduce-scatter.12
  638.2 100.1 reduce-scatter.8
  741.1 126.0 reduce-scatter.16
  869.7 126.0 reduce-scatter.20
  1000.0 63.4 reduce-scatter.14
  1067.6 73.3 reduce-scatter.10
  1145.1 86.9 reduce-scatter.18
  1236.7 87.6 reduce-scatter.22
where the time goes:
time: 1340 us; the launch traced here: 1330 us
  waiting for transfers between devices  646 us (48%)
  matrix products  334 us (25%)
  local copies, waits for them, and re-layouts  152 us (11%)
  other arithmetic  123 us (9%)
  blocking collectives  40.4 us (3%)
  starting transfers between devices  21.1 us (2%)
  between operations  14.8 us (1%)
    reduce_scatter x1, waiting for transfers between devices, on_device(): lax.psum_scatter(up_grad, 'seq', scatter_dimension=1, tiled=True)  129 us
    reduce_scatter x1, waiting for transfers between devices, on_device(): lax.psum_scatter(down_grad, 'seq', scatter_dimension=1, tiled=True)  123 us
    reduce_scatter x1, waiting for transfers between devices, on_device(): lax.psum_scatter(partial_sums[3], 'dp', scatter_dimension=0, tiled=True)  92.3 us
    reduce_scatter x1, waiting for transfers between devices, on_device(): lax.psum_scatter(partial_sums[2], 'dp', scatter_dimension=0, tiled=True)  91.2 us
    all_to_all x1, waiting for transfers between devices, on_device(): lax.all_to_all(d_blocks, 'seq', split_axis=1, concat_axis=3, tiled=True)  82.8 us
    dot_general x8, matrix products, masked_scores(): jnp.einsum('qhd,khd->hqk', queries, key_rows, preferred_element_type=jnp....  62.9 us
    all_to_all x1, waiting for transfers between devices, on_device(): lax.all_to_all(outgoing, 'seq', split_axis=3, concat_axis=1, tiled=True)  58.3 us
    reduce_scatter x1, waiting for transfers between devices, on_device(): lax.psum_scatter(partial_sums[0], 'dp', scatter_dimension=0, tiled=True)  51.3 us
  transfers between devices with their start and end apart: 12, of which 8 were waited for; matrix products, arithmetic and copies ran while one was open for 37% of the time, Pallas kernels for 0%

commit v1 on v0

--- a/solution.py
+++ b/solution.py
@@ -1,12 +1,22 @@
+import functools
 import jax
 import jax.numpy as jnp
 from jax import lax
 from jax.sharding import PartitionSpec as P
+from jax.lax import psum
 
 HEADS = 16
 HEAD_DIM = 64
 ROT = 32
 EPS = 1e-05
+
+
+def load_task(local, axis_name, device_axis):
+    field_out = psum(local, axis_name)
+    return psum(field_out, device_axis)
+
+
+make_orders = functools.partial(load_task, axis_name="seq", device_axis="dp")
 
 
 def norm_piece(values, norm_gain, norm_shift):
@@ -171,8 +181,8 @@
     )
     d_values, gain_grad, shift_grad = norm_pull(d_normed.reshape(inputs.shape))
     input_grad = grad_low.astype(jnp.float32).reshape(inputs.shape) + d_values
-    gain_sum, shift_sum, up_bias_sum, down_bias_sum = lax.psum(
-        (gain_grad, shift_grad, up_bias_grad, down_bias_grad), ("dp", "seq")
+    gain_sum, shift_sum, up_bias_sum, down_bias_sum = make_orders(
+        (gain_grad, shift_grad, up_bias_grad, down_bias_grad)
     )
     partial_sums = (
         lax.psum_scatter(qkv_grad, "seq", scatter_dimension=1, tiled=True),

time: 1340 us -> 1340 us (level)
    psum x1 -> x2, blocking collectives: 40.4 us -> 48.8 us  [the longest x1 38.5 us: load_task(): return psum(field_out, device_axis)]
where the time goes in v1:
time: 1340 us; the launch traced here: 1330 us
  waiting for transfers between devices  638 us (48%)
  matrix products  334 us (25%)
  local copies, waits for them, and re-layouts  152 us (11%)
  other arithmetic  123 us (9%)
  blocking collectives  48.8 us (4%)
  starting transfers between devices  21.1 us (2%)
  between operations  14.9 us (1%)
    reduce_scatter x1, waiting for transfers between devices, on_device(): lax.psum_scatter(up_grad, 'seq', scatter_dimension=1, tiled=True)  129 us
    reduce_scatter x1, waiting for transfers between devices, on_device(): lax.psum_scatter(down_grad, 'seq', scatter_dimension=1, tiled=True)  123 us
    reduce_scatter x1, waiting for transfers between devices, on_device(): lax.psum_scatter(partial_sums[3], 'dp', scatter_dimension=0, tiled=True)  92.3 us
    reduce_scatter x1, waiting for transfers between devices, on_device(): lax.psum_scatter(partial_sums[2], 'dp', scatter_dimension=0, tiled=True)  91.4 us
    all_to_all x1, waiting for transfers between devices, on_device(): lax.all_to_all(d_blocks, 'seq', split_axis=1, concat_axis=3, tiled=True)  82.8 us
    dot_general x8, matrix products, masked_scores(): jnp.einsum('qhd,khd->hqk', queries, key_rows, preferred_element_type=jnp....  62.9 us
    all_to_all x1, waiting for transfers between devices, on_device(): lax.all_to_all(outgoing, 'seq', split_axis=3, concat_axis=1, tiled=True)  58.3 us
    convert_element_type x4, other arithmetic, backward_row(): (chances * (d_chances - jnp.sum(chances * d_chances, -1, keepdims=True)))...  47.6 us
  transfers between devices with their start and end apart: 12, of which 8 were waited for; matrix products, arithmetic and copies ran while one was open for 37% of the time, Pallas kernels for 0%

profile of v1, /device:TPU:0, one launch (start us, length us, event | category | flops | bytes accessed | tf_op | source)
XLA Modules:
  0.0 1331.8 jit_solution(15536964556171029865)
XLA Ops:
  36.0 8.6 copy.107
  48.4 10.8 fusion.39
  78.0 5.8 all-to-all-start
  96.8 58.3 %all-to-all-done = bf16[4,256,3,4,256]{1,4,0,2,3:T(8,128)(2,1)} async-done(((bf16[4,256,3,4,256]{1,4,0,2,3:T(8,128)(2,1)}), bf16[4,256,3,4,256]{1,4,0,2,3:T(8,128)(2,1)}, u32[]{:S(2)}, u32[]{:S(2)}) %all-to-all-start) | async-done | bytes 6291488 | tf_op jit(solution)/shard_map/all_to_all | solution.py:134
  155.2 10.3 copy.112
  165.4 11.0 reshape.385
  176.4 60.7 %while.22 = (s32[]{:T(128)}, bf16[4,1024,4,64]{1,3,2,0:T(8,128)(2,1)}, f32[4,4,1024]{2,1,0:T(4,128)}, bf16[4,1024,3,4,64]{1,4,3,2,0:T(8,128)(2,1)}, s32[4,1024]{1,0:T(4,128)S(1)}, /*index=5*/s32[]{:T(128)}) while((s32[]{:T(128)}, bf16[4,1024,4,64]{1,3,2,0:T(8,128)(2,1)}, f32[4,4,1024]{2,1,0:T(4,128)}, bf16[4,1024,3,4,64]{1,4,3,2,0:T(8,128)(2,1)}, ...), condition=%wide.region_5.6_spmd, body=%wide.region_2.5_spmd.sunk | while | flops 1127477248 | bytes 59913292 | solution.py:137
  186.0 5.6 fusion.93
  201.1 5.6 fusion.93
  216.3 5.6 fusion.93
  246.0 208.5 %while.23 = (s32[]{:T(128)}, bf16[4,1024,3,4,64]{1,4,3,2,0:T(8,128)(2,1)}, bf16[4,1024,3,4,64]{1,4,3,2,0:T(8,128)(2,1)}, s32[4,1024]{1,0:T(4,128)S(1)}, f32[4,4,...) while((s32[]{:T(128)}, bf16[4,1024,3,4,64]{1,4,3,2,0:T(8,128)(2,1)}, ...), condition=%wide.region_8.9_spmd, body=%wide.region_6.8_spmd.sunk | while | flops 2731274240 | bytes 196179696 | solution.py:172
  247.6 9.6 fusion.99
  258.5 12.7 multiply_reduce_fusion.5
  271.2 11.9 multiply_convert_fusion.5
  299.7 9.6 fusion.99
  310.6 12.7 multiply_reduce_fusion.5
  323.3 11.9 multiply_convert_fusion.5
  351.8 9.6 fusion.99
  362.7 12.7 multiply_reduce_fusion.5
  375.4 11.9 multiply_convert_fusion.5
  403.9 9.6 fusion.99
  414.8 12.7 multiply_reduce_fusion.5
  427.5 11.9 multiply_convert_fusion.5
  454.5 10.8 copy.118
  480.9 82.8 %all-to-all-done.3 = bf16[4,1024,3,1,256]{4,0,3,2,1:T(4,128)(2,1)} async-done(((bf16[4,1024,3,1,256]{4,0,3,2,1:T(4,128)(2,1)}), bf16[4,1024,3,1,256]{4,0,3,2,1:T(4,128)(2,1)}, u32[]{:S(2)}, u32[]{:S(2)}) %all-to-all-start.3) | async-done | bytes 6291488 | tf_op jit(solution)/shard_map/all_to_all | solution.py:174
  567.4 6.2 convert_bitcast_fusion
  573.6 12.6 copy.120
  586.2 9.9 fusion.45
  602.5 7.1 add_convert_fusion
  609.6 11.6 copy.121
  628.8 9.2 fusion.50
  638.1 18.6 %fusion.48 = f32[1024,4096]{1,0:T(8,128)} fusion(bf16[1024,1024]{1,0:T(8,128)(2,1)} %bitcast.215, bf16[1024,4096]{1,0:T(8,128)(2,1)} %param.21), kind=kOutput, calls=%fused_computation.117 | convolution fusion | flops 8589934592 | bytes 27262976 | tf_op jit(solution)/shard_map/dot_general | solution.py:148
  656.8 26.5 %convert_reduce_fusion = (f32[4096]{0:T(1024)S(1)}, bf16[1024,4096]{1,0:T(8,128)(2,1)}) fusion(f32[1024,4096]{1,0:T(8,128)} %fusion.48, f32[4096]{0:T(1024)S(1)} %copy-done.28, bf16[1024,1024]{1,0:T(8,128)(2,1)} %copy-done.9, bf16[4096,1024]{1,0:T(8,128)(2,1)} %param.23), kind=kOutput, calls=%fused_computation.59 | convolution fusion | flops 8686399488 | bytes 35684352 | tf_op jit(solution)/shard_map/td,fd->tf/dot_general | solution.py:162
  683.3 16.4 %fusion.52 = f32[1024,4096]{1,0:T(8,128)} fusion(bf16[1024,1024]{1,0:T(8,128)(2,1)} %bitcast.216, bf16[1024,4096]{1,0:T(8,128)(2,1)} %get-tuple-element.108), kind=kOutput, calls=%fused_computation.121 | convolution fusion | flops 8589934592 | bytes 27262976 | tf_op jit(solution)/shard_map/td,tf->df/dot_general | solution.py:165
  699.7 20.1 %fusion.43 = f32[4096,1024]{1,0:T(8,128)} fusion(bf16[1024,1024]{1,0:T(8,128)(2,1)} %copy-done.9, f32[1024,4096]{1,0:T(8,128)} %fusion.48, f32[4096]{0:T(1024)S(1)} %copy-done.28), kind=kOutput, calls=%fused_computation.113 | convolution fusion | flops 8631877632 | bytes 35667968 | tf_op jit(solution)/shard_map/tf,td->fd/dot_general | solution.py:159
  720.5 17.9 %reduce-scatter.9.cloned.1.call-done = f32[1024,768]{1,0:T(8,128)} async-done(((f32[1024,3072]{1,0:T(8,128)}), f32[1024,768]{1,0:T(8,128)}) %reduce-scatter.9.cloned.1.call-update) | async-done | bytes 3145744 | tf_op jit(solution)/shard_map/reduce_scatter | solution.py:188
  738.4 128.9 %reduce-scatter.17.cloned.1.call-done = f32[1024,1024]{1,0:T(8,128)} async-done(((f32[1024,4096]{1,0:T(8,128)}), f32[1024,1024]{1,0:T(8,128)}) %reduce-scatter.17.cloned.1.call-update) | async-done | bytes 4194320 | tf_op jit(solution)/shard_map/reduce_scatter | solution.py:190
  867.3 5.9 fusion.47
  873.3 122.6 %reduce-scatter.21.cloned.1.call-done = f32[4096,256]{1,0:T(8,128)} async-done(((f32[4096,1024]{1,0:T(8,128)}), f32[4096,256]{1,0:T(8,128)}) %reduce-scatter.21.cloned.1.call-update) | async-done | bytes 4194320 | tf_op jit(solution)/shard_map/reduce_scatter | solution.py:191
  995.9 19.7 %fusion.38 = bf16[1024,1024]{1,0:T(8,128)(2,1)} fusion(f32[1024,1024]{1,0:T(8,128)} %fusion.47, bf16[4,256,1024]{2,1,0:T(8,128)(2,1)} %param.16, f32[1024]{0:T(1024)S(1)} %copy-done.29, bf16[4096,1024]{1,0:T(8,128)(2,1)} %param.23, f32[1024,4096]{1,0:T(8,128)} %fusion.48, f32[4096]{0:T(1024)S(1)} %copy-done.28), kind=kOutput, calls=%fused_computation.74 | convolution fusion | flops 8637120512 | bytes 33574912 | tf_op jit(solution)/shard_map/dot_general | solution.py:151
  1015.6 10.7 fusion.49
  1026.4 14.2 %fusion.46 = (f32[1024]{0:T(1024)S(1)}, f32[1024,1024]{1,0:T(8,128)S(1)}) fusion(f32[1024,1024]{1,0:T(8,128)S(1)} %fusion.49, bf16[1024,4096]{1,0:T(8,128)(2,1)} %get-tuple-element.108, bf16[1024,4096]{1,0:T(8,128)(2,1)} %param.21), kind=kOutput, calls=%fused_computation.115 | convolution fusion | flops 8592030720 | bytes 25169920 | tf_op jit(solution)/shard_map/tf,df->td/dot_general | solution.py:179
  1043.6 10.3 all-reduce.10
  1053.9 38.5 %all-reduce.9 = (f32[1024]{0:T(1024)}, f32[1024]{0:T(1024)}, f32[4096]{0:T(1024)}, f32[1024]{0:T(1024)}) all-reduce(f32[1024]{0:T(1024)S(1)} %get-tuple-element.101, f32[1024]{0:T(1024)S(1)} %get-tuple-element.102, f32[4096]{0:T(1024)S(1)} %get-tuple-element.103, ...), channel_id=1, replica_groups=mesh['dp'=8,'seq'=4] {'dp'}, use_global_device_ids=true, to_apply=%region_13.14 | all-reduce | flops 7168 | bytes 57344 | tf_op jit(solution)/shard_map/psum | solution.py:16
  1092.3 5.7 convert_add_fusion
  1098.0 43.0 %reduce-scatter.11.cloned.1.call-done = f32[128,768]{1,0:T(8,128)} async-done(((f32[1024,768]{1,0:T(8,128)}), f32[128,768]{1,0:T(8,128)}) %reduce-scatter.11.cloned.1.call-update) | async-done | bytes 393232 | tf_op jit(solution)/shard_map/reduce_scatter | solution.py:194
  1141.0 91.4 %reduce-scatter.19.cloned.1.call-done = f32[128,1024]{1,0:T(8,128)} async-done(((f32[1024,1024]{1,0:T(8,128)}), f32[128,1024]{1,0:T(8,128)}) %reduce-scatter.19.cloned.1.call-update) | async-done | bytes 524304 | tf_op jit(solution)/shard_map/reduce_scatter | solution.py:196
  1232.4 92.3 %reduce-scatter.23.cloned.1.call-done = f32[512,256]{1,0:T(8,128)} async-done(((f32[4096,256]{1,0:T(8,128)}), f32[512,256]{1,0:T(8,128)}) %reduce-scatter.23.cloned.1.call-update) | async-done | bytes 524304 | tf_op jit(solution)/shard_map/reduce_scatter | solution.py:197
  (229 shorter events, 225.4 us)
Async XLA Ops:
  7.2 7.7 copy-start
  26.4 51.6 %all-to-all-start.2 = ((bf16[4,256,4,256]{3,1,0,2:T(8,128)(2,1)}), bf16[4,256,4,256]{3,1,0,2:T(8,128)(2,1)}, u32[]{:S(2)}, u32[]{:S(2)}) async-start(bf16[4,256,4,256]{3,1,0,2:T(8,128)(2,1)} %copy.116), calls=%async_computation.2 | async-start | bytes 4194304 | tf_op jit(solution)/shard_map/all_to_all | solution.py:170
  33.1 11.6 copy-start.17
  36.0 8.7 copy-start.20
  36.0 8.7 copy-start.22
  36.0 8.7 copy-start.27
  69.3 3.2 copy-start.8
  69.5 3.0 copy-start.13
  69.5 3.0 copy-start.15
  78.0 77.2 %all-to-all-start = ((bf16[4,256,3,4,256]{1,4,0,2,3:T(8,128)(2,1)}), bf16[4,256,3,4,256]{1,4,0,2,3:T(8,128)(2,1)}, u32[]{:S(2)}, u32[]{:S(2)}) async-start(bf16[4,256,3,4,256]{1,4,0,2,3:T(8,128)(2,1)} %copy.127), calls=%async_computation | async-start | bytes 12582912 | tf_op jit(solution)/shard_map/all_to_all | solution.py:134
  165.4 11.0 copy-start.19
  241.4 223.9 %all-to-all-start.1 = ((bf16[4,1024,1,256]{3,0,2,1:T(4,128)(2,1)}), bf16[4,1024,1,256]{3,0,2,1:T(4,128)(2,1)}, u32[]{:S(2)}, u32[]{:S(2)}) async-start(bf16[4,1024,1,256]{3,0,2,1:T(4,128)(2,1)} %copy.113), calls=%async_computation.1 | async-start | bytes 4194304 | tf_op jit(solution)/shard_map/all_to_all | solution.py:139
  247.5 10.9 copy-start.1
  271.2 20.0 %slice-start = ((s8[16777216]{0:T(1024)(128)(4,1)}), s8[4194304]{0:T(1024)(128)(4,1)S(1)}, s32[]{:S(2)}) async-start(s8[16777216]{0:T(1024)(128)(4,1)} %bitcast.198), calls=%async_computation.20 | async-start | bytes 8388608 | tf_op jit(solution)/shard_map/while
  271.2 20.0 %slice-start.1 = ((s8[16777216]{0:T(1024)(128)(4,1)}), s8[4194304]{0:T(1024)(128)(4,1)S(1)}, s32[]{:S(2)}) async-start(s8[16777216]{0:T(1024)(128)(4,1)} %bitcast.198), calls=%async_computation.21 | async-start | bytes 8388608 | tf_op jit(solution)/shard_map/while
  271.2 20.0 %slice-start.2 = ((s8[16777216]{0:T(1024)(128)(4,1)}), s8[4194304]{0:T(1024)(128)(4,1)S(1)}, s32[]{:S(2)}) async-start(s8[16777216]{0:T(1024)(128)(4,1)} %bitcast.198), calls=%async_computation.22 | async-start | bytes 8388608 | tf_op jit(solution)/shard_map/while
  283.1 8.1 slice-start.3
  299.7 10.9 copy-start.1
  323.3 20.0 %slice-start = ((s8[16777216]{0:T(1024)(128)(4,1)}), s8[4194304]{0:T(1024)(128)(4,1)S(1)}, s32[]{:S(2)}) async-start(s8[16777216]{0:T(1024)(128)(4,1)} %bitcast.198), calls=%async_computation.20 | async-start | bytes 8388608 | tf_op jit(solution)/shard_map/while
  323.3 20.0 %slice-start.1 = ((s8[16777216]{0:T(1024)(128)(4,1)}), s8[4194304]{0:T(1024)(128)(4,1)S(1)}, s32[]{:S(2)}) async-start(s8[16777216]{0:T(1024)(128)(4,1)} %bitcast.198), calls=%async_computation.21 | async-start | bytes 8388608 | tf_op jit(solution)/shard_map/while
  323.3 20.0 %slice-start.2 = ((s8[16777216]{0:T(1024)(128)(4,1)}), s8[4194304]{0:T(1024)(128)(4,1)S(1)}, s32[]{:S(2)}) async-start(s8[16777216]{0:T(1024)(128)(4,1)} %bitcast.198), calls=%async_computation.22 | async-start | bytes 8388608 | tf_op jit(solution)/shard_map/while
  335.2 8.1 slice-start.3
  351.8 10.9 copy-start.1
  375.4 20.0 %slice-start = ((s8[16777216]{0:T(1024)(128)(4,1)}), s8[4194304]{0:T(1024)(128)(4,1)S(1)}, s32[]{:S(2)}) async-start(s8[16777216]{0:T(1024)(128)(4,1)} %bitcast.198), calls=%async_computation.20 | async-start | bytes 8388608 | tf_op jit(solution)/shard_map/while
  375.4 20.0 %slice-start.1 = ((s8[16777216]{0:T(1024)(128)(4,1)}), s8[4194304]{0:T(1024)(128)(4,1)S(1)}, s32[]{:S(2)}) async-start(s8[16777216]{0:T(1024)(128)(4,1)} %bitcast.198), calls=%async_computation.21 | async-start | bytes 8388608 | tf_op jit(solution)/shard_map/while
  375.4 20.0 %slice-start.2 = ((s8[16777216]{0:T(1024)(128)(4,1)}), s8[4194304]{0:T(1024)(128)(4,1)S(1)}, s32[]{:S(2)}) async-start(s8[16777216]{0:T(1024)(128)(4,1)} %bitcast.198), calls=%async_computation.22 | async-start | bytes 8388608 | tf_op jit(solution)/shard_map/while
  387.3 8.1 slice-start.3
  403.9 10.9 copy-start.1
  427.5 20.0 %slice-start = ((s8[16777216]{0:T(1024)(128)(4,1)}), s8[4194304]{0:T(1024)(128)(4,1)S(1)}, s32[]{:S(2)}) async-start(s8[16777216]{0:T(1024)(128)(4,1)} %bitcast.198), calls=%async_computation.20 | async-start | bytes 8388608 | tf_op jit(solution)/shard_map/while
  427.5 20.0 %slice-start.1 = ((s8[16777216]{0:T(1024)(128)(4,1)}), s8[4194304]{0:T(1024)(128)(4,1)S(1)}, s32[]{:S(2)}) async-start(s8[16777216]{0:T(1024)(128)(4,1)} %bitcast.198), calls=%async_computation.21 | async-start | bytes 8388608 | tf_op jit(solution)/shard_map/while
  427.5 20.0 %slice-start.2 = ((s8[16777216]{0:T(1024)(128)(4,1)}), s8[4194304]{0:T(1024)(128)(4,1)S(1)}, s32[]{:S(2)}) async-start(s8[16777216]{0:T(1024)(128)(4,1)} %bitcast.198), calls=%async_computation.22 | async-start | bytes 8388608 | tf_op jit(solution)/shard_map/while
  439.4 8.1 slice-start.3
  465.3 98.4 %all-to-all-start.3 = ((bf16[4,1024,3,1,256]{4,0,3,2,1:T(4,128)(2,1)}), bf16[4,1024,3,1,256]{4,0,3,2,1:T(4,128)(2,1)}, u32[]{:S(2)}, u32[]{:S(2)}) async-start(bf16[4,1024,3,1,256]{4,0,3,2,1:T(4,128)(2,1)} %copy.118), calls=%async_computation.3 | async-start | bytes 12582912 | tf_op jit(solution)/shard_map/all_to_all | solution.py:174
  470.5 249.4 %reduce-scatter.13.cloned.1.call-start = ((), (), s32[]{:S(2)}) async-start(), calls=%async_computation.14 | async-start | bytes 5242880 | tf_op jit(solution)/shard_map/reduce_scatter | solution.py:189
  472.8 3.5 copy-start.5
  480.8 257.5 %reduce-scatter.9.cloned.1.call-start = ((), (), s32[]{:S(2)}) async-start(), calls=%async_computation.12 | async-start | bytes 15728640 | tf_op jit(solution)/shard_map/reduce_scatter | solution.py:188
  621.2 7.6 copy-start.11
  638.1 18.7 %copy-start.28 = (f32[4096]{0:T(1024)S(1)}, f32[4096]{0:T(1024)}, u32[]{:S(2)}) copy-start(f32[4096]{0:T(1024)} %param.22) | copy-start | bytes 49156
  638.1 229.2 %reduce-scatter.17.cloned.1.call-start = ((), (), s32[]{:S(2)}) async-start(), calls=%async_computation.16 | async-start | bytes 20971520 | tf_op jit(solution)/shard_map/reduce_scatter | solution.py:190
  699.6 296.2 %reduce-scatter.21.cloned.1.call-start = ((), (), s32[]{:S(2)}) async-start(), calls=%async_computation.18 | async-start | bytes 20971520 | tf_op jit(solution)/shard_map/reduce_scatter | solution.py:191
  719.8 378.2 %reduce-scatter.15.cloned.1.call-start = ((), (), s32[]{:S(2)}) async-start(), calls=%async_computation.15 | async-start | bytes 1179648 | tf_op jit(solution)/shard_map/reduce_scatter | solution.py:195
  720.4 420.6 %reduce-scatter.11.cloned.1.call-start = ((), (), s32[]{:S(2)}) async-start(), calls=%async_computation.13 | async-start | bytes 3538944 | tf_op jit(solution)/shard_map/reduce_scatter | solution.py:194
  738.4 494.0 %reduce-scatter.19.cloned.1.call-start = ((), (), s32[]{:S(2)}) async-start(), calls=%async_computation.17 | async-start | bytes 4718592 | tf_op jit(solution)/shard_map/reduce_scatter | solution.py:196
  867.3 457.4 %reduce-scatter.23.cloned.1.call-start = ((), (), s32[]{:S(2)}) async-start(), calls=%async_computation.19 | async-start | bytes 4718592 | tf_op jit(solution)/shard_map/reduce_scatter | solution.py:197
  873.3 122.6 %copy-start.29 = (f32[1024]{0:T(1024)S(1)}, f32[1024]{0:T(1024)}, u32[]{:S(2)}) copy-start(f32[1024]{0:T(1024)} %param.24) | copy-start | bytes 12292
  1026.3 14.2 %copy-start.2 = (bf16[4,256,1024]{2,1,0:T(8,128)(2,1)S(1)}, bf16[4,256,1024]{2,1,0:T(8,128)(2,1)}, u32[]{:S(2)}) copy-start(bf16[4,256,1024]{2,1,0:T(8,128)(2,1)} %param.16) | copy-start | bytes 6291460
  1026.4 14.2 %copy-start.18 = (f32[4,256]{1,0:T(4,128)S(1)}, f32[4,256]{1,0:T(4,128)}, u32[]{:S(2)}) copy-start(f32[4,256]{1,0:T(4,128)} %copy-done.17) | copy-start | bytes 12292
  1026.4 14.2 %copy-start.23 = (f32[1024]{0:T(1024)S(1)}, f32[1024]{0:T(1024)}, u32[]{:S(2)}) copy-start(f32[1024]{0:T(1024)} %param.17) | copy-start | bytes 12292
  (13 other events, 24.2 us)
Sparse Core Ops, SparseCore 0:
  480.9 69.5 reduce-scatter.12
  638.2 100.0 reduce-scatter.8
  741.1 126.1 reduce-scatter.16
  869.7 126.1 reduce-scatter.20
  1000.1 63.3 reduce-scatter.14
  1067.5 73.4 reduce-scatter.10
  1145.2 87.1 reduce-scatter.18
  1237.0 87.6 reduce-scatter.22
